TPU v7x, 128 devices: a whole 4x4x4 slice. The times are simulated.
128 devices in a mesh: shot: 32 (over x_lo, z, y), freq: 4 (over x_hi, core).
Axes of the slice: x: 4 (x_hi: 2, x_lo: 2; x = x_hi * 2 + x_lo), y: 4, z: 4, core: 2. Of those that a mesh axis runs over, the one named last changes fastest.
Arguments:
- recorded: bfloat16 [2, 256, 2048, 512], P(None, 'freq', 'shot'), may hold values from -6 to 6
- rec_shot: int32 [2048, 512], P('shot'), may hold values from 0 to 2047
- owners: int32 [3], replicated, may hold values from 0 to 31, as said below
Outputs:
- primaries: bfloat16 [2048, 512, 512], P('shot', 'freq')
- filters: float32 [2048, 31], P('shot')
Inputs may be any that keep to these rules, and one draw needn't show every extreme that they name: The 3 owners are distinct; the first and the last index of the shot axis are always among them.
All inputs are finite; a program needn't handle non-finite values.
Results may differ from a plain program's by a relative error of at most 0.008.
Values may be sent and summed in bfloat16 or wider, within the bound.
A program may use at most 192 MiB of HBM per device.

v0:
```python
import math
import jax
import jax.numpy as jnp
from jax import lax
from jax.sharding import PartitionSpec as P

F = 256
TAPS = 31
STEPS = 3
REG = 2.0


def broadcast(value, axis, source):
    kept = jnp.where(lax.axis_index(axis) == source, value, 0).astype(value.dtype)
    return lax.psum(kept, axis)


def angles(freq_index, step_index, period):
    product_mod = jnp.mod(freq_index[:, None] * step_index[None, :], period)
    return product_mod.astype(jnp.float32) * (2.0 * math.pi / period)


def solve_filters(autocorr, crosscorr, tap_count, damping):
    half_taps = (tap_count - 1) // 2
    tap_index = jnp.arange(tap_count, dtype=jnp.int32)
    distance = jnp.abs(tap_index[:, None] - tap_index[None, :])
    normal = autocorr[:, distance] + damping * jnp.eye(tap_count, dtype=jnp.float32)[None, :, :]
    target = crosscorr + damping * (tap_index == half_taps).astype(jnp.float32)[None, :]
    factor = jnp.linalg.cholesky(normal)
    middle = lax.linalg.triangular_solve(factor, target[:, :, None], left_side=True, lower=True)
    solved = lax.linalg.triangular_solve(
        factor, middle, left_side=True, lower=True, transpose_a=True
    )
    return solved[:, :, 0]


def band_table(freq_index, freq_count):
    period = 2 * freq_count
    phase_angles = angles(freq_index, jnp.arange(period, dtype=jnp.int32), period)
    norm_factor = 1.0 / math.sqrt(freq_count)
    return jnp.stack(
        [jnp.cos(phase_angles) * norm_factor, -jnp.sin(phase_angles) * norm_factor]
    ).astype(jnp.bfloat16)


def fetch_owner(data_slab, owner):
    return broadcast(data_slab, "shot", owner)


def product_step(data_slab, rec_shot, owner, owner_block):
    shot_count = data_slab.shape[2]
    offset_index = rec_shot - owner * shot_count
    slot_keys = jnp.arange(shot_count, dtype=jnp.int32)
    one_hot = (offset_index[:, None, :] == slot_keys[None, :, None]).astype(jnp.bfloat16)
    coeffs = jnp.einsum(
        "cfsr,skr->cfsk", data_slab, one_hot, preferred_element_type=jnp.float32
    ).astype(jnp.bfloat16)
    left_real = jnp.concatenate([coeffs[0], -coeffs[1]], axis=2)
    left_imag = jnp.concatenate([coeffs[1], coeffs[0]], axis=2)
    stacked = jnp.stack([left_real, left_imag])
    right_side = jnp.concatenate([owner_block[0], owner_block[1]], axis=1)
    return jnp.einsum("cfsk,fkr->cfsr", stacked, right_side, preferred_element_type=jnp.float32)


def per_device(recorded, rec_shot, owners):
    band_count = recorded.shape[1]
    recv_count = recorded.shape[3]
    half_taps = (TAPS - 1) // 2
    summed = jnp.zeros(recorded.shape, jnp.float32)
    for step_index in range(STEPS):
        owner_block = fetch_owner(recorded, owners[step_index])
        summed = summed + product_step(recorded, rec_shot, owners[step_index], owner_block)
    pred_gain = (lax.axis_size("shot") / (2.0 * recv_count * STEPS)) ** 0.5
    predicted = (pred_gain * summed).astype(jnp.bfloat16)
    pred_wide = predicted.astype(jnp.float32)
    data_wide = recorded.astype(jnp.float32)
    spectrum = jnp.sum(pred_wide[0] * pred_wide[0] + pred_wide[1] * pred_wide[1], axis=2)
    cross_real = jnp.sum(pred_wide[0] * data_wide[0] + pred_wide[1] * data_wide[1], axis=2)
    cross_imag = jnp.sum(pred_wide[0] * data_wide[1] - pred_wide[1] * data_wide[0], axis=2)
    highest = lax.Precision.HIGHEST
    freq_index = lax.axis_index("freq") * band_count + jnp.arange(band_count, dtype=jnp.int32)
    tap_index = jnp.arange(TAPS, dtype=jnp.int32)
    lag_angles = angles(freq_index, tap_index, 2 * F)
    tap_angles = angles(freq_index, tap_index - half_taps, 2 * F)
    auto_part = jnp.dot(spectrum.T, jnp.cos(lag_angles), precision=highest)
    cross_part = jnp.dot(cross_real.T, jnp.cos(tap_angles), precision=highest) - jnp.dot(
        cross_imag.T, jnp.sin(tap_angles), precision=highest
    )
    autocorr, crosscorr = lax.psum((auto_part, cross_part), "freq")
    filters = solve_filters(autocorr, crosscorr, TAPS, REG * recv_count * F)
    resp_real = jnp.dot(jnp.cos(tap_angles), filters.T, precision=highest)[:, :, None]
    resp_imag = -jnp.dot(jnp.sin(tap_angles), filters.T, precision=highest)[:, :, None]
    res_real = data_wide[0] - (resp_real * pred_wide[0] - resp_imag * pred_wide[1])
    res_imag = data_wide[1] - (resp_real * pred_wide[1] + resp_imag * pred_wide[0])
    residual = jnp.stack([res_real, res_imag]).astype(jnp.bfloat16)
    full_table = band_table(jnp.arange(F, dtype=jnp.int32), F).reshape(2 * F, 2 * F)
    shard_piece = lax.all_to_all(residual, "freq", split_axis=3, concat_axis=1, tiled=True)
    item_count = shard_piece.shape[2]
    recv_part = shard_piece.shape[3]
    flattened = shard_piece.reshape(2 * F, item_count * recv_part)
    time_rows = lax.dot_general(
        flattened, full_table, (((0,), (0,)), ((), ())), preferred_element_type=jnp.float32
    )
    primaries = time_rows.reshape(item_count, recv_part, 2 * F).astype(jnp.bfloat16)
    return (primaries, filters)


def solution(mesh):
    placed = (P(None, "freq", "shot", None), P("shot", None), P())
    return jax.shard_map(
        per_device,
        mesh=mesh,
        in_specs=placed,
        out_specs=(P("shot", "freq", None), P("shot", None)),
        check_vma=False,
    )
```

profile of v0, /device:TPU:1, one launch (start us, length us, event | category | flops | bytes accessed | tf_op | source)
XLA Modules:
  0.0 1144.3 jit_solution(10621958001166463618)
XLA Ops:
  10.5 11.0 broadcast_select_fusion.1
  23.4 11.5 %copy.36 = bf16[2,64,64,512]{3,1,0,2:T(8,128)(2,1)} copy(bf16[2,64,64,512]{3,2,1,0:T(8,128)(2,1)} %param.3) | data formatting | bytes 16777216 | tf_op args[0]
  35.2 5.7 fusion.9
  42.9 1.5 pad_maximum_fusion.2
  45.8 2.3 fusion.8
  50.4 1.5 pad_maximum_fusion.1
  51.9 2.3 fusion.10
  56.2 1.5 pad_maximum_fusion.3
  57.8 11.7 %copy_convert_fusion = f32[2,64,64,512]{3,2,0,1:T(8,128)} fusion(bf16[2,64,64,512]{3,2,1,0:T(8,128)(2,1)} %param.3), kind=kLoop, calls=%fused_computation.16 | loop fusion | flops 4194304 | bytes 25165824 | tf_op jit(solution)/shard_map/convert_element_type | solution.py:76
  69.5 510.7 %all-reduce.4.cloned.1.call-done = (bf16[2,64,64,512]{3,2,1,0:T(8,128)(2,1)}, bf16[2,64,64,512]{3,2,1,0:T(8,128)(2,1)}, bf16[2,64,64,512]{3,2,1,0:T(8,128)(2,1)}) async-done(((bf16[2,64,64,512]{3,2,1,0:T(8,128)(2,1)}, bf16[2,64,64,512]{3,2,1,0:T(8,128)(2,1)}, bf16[2,64,64,512]{3,2,1,0:T(8,128)(2,1)}), (bf16[2,64,64,512]{3,2,1,0:T(8,128)(2,1)}, bf16[2,64,64,512]{3,2,1,0:T(8,128)(2,1)}, ...) | async-done | bytes 25165840 | tf_op jit(solution)/shard_map/psum | solution.py:15
  580.2 4.0 slice_bitcast_fusion.5
  584.2 11.2 slice_bitcast_fusion.1
  595.4 10.3 fusion.3
  605.7 10.2 fusion
  615.8 20.8 %convert_bitcast_fusion = f32[2,64,64,512]{3,2,0,1:T(8,128)} fusion(bf16[64,64,512]{2,1,0:T(8,128)(2,1)} %get-tuple-element.17, bf16[64,64,512]{2,1,0:T(8,128)(2,1)S(1)} %copy-done, f32[64,512,2,64]{1,3,2,0:T(8,128)} %fusion, f32[64,512,2,64]{1,3,2,0:T(8,128)} %fusion.3, bf16[2,64,64,128]{3,1,2,0:T(8,128)(2,1)} %pad_maximum_fusion.3), kind=kOutput, calls=%fused_computation.1 | convolution fusion | flops 1111490560 | bytes 60817408 | tf_op jit(solution)/shard_map/cfsk,fkr->cfsr/dot_general | solution.py:62
  636.7 13.9 %subtract_reduce_fusion = (f32[64,64]{1,0:T(8,128)S(1)}, f32[64,64]{1,0:T(8,128)S(1)}, f32[64,64]{1,0:T(8,128)S(1)}) fusion(f32[2,64,64,512]{3,2,0,1:T(8,128)} %copy_convert_fusion, f32[2,64,64,512]{3,2,0,1:T(8,128)} %convert_bitcast_fusion), kind=kLoop, calls=%fused_computation.19 | loop fusion | flops 25153536 | bytes 33603584 | tf_op jit(solution)/shard_map/reduce_sum | solution.py:79
  651.8 13.8 %all-reduce = (f32[64,31]{0,1:T(8,128)S(1)}, f32[64,31]{0,1:T(8,128)S(1)}) all-reduce(f32[64,31]{0,1:T(8,128)S(1)} %fusion.33, f32[64,31]{0,1:T(8,128)S(1)} %convolution_subtract_fusion), channel_id=1, replica_groups=mesh['shot'=32,'freq'=4] {'freq'}, use_global_device_ids=true, to_apply=%region_4.5 | all-reduce | flops 3968 | bytes 31744 | tf_op jit(solution)/shard_map/psum | solution.py:89
  665.6 2.9 gather_fusion
  671.7 182.3 %custom-call.9 = f32[64,31,31]{2,1,0:T(8,128)S(1)} custom-call(f32[64,31,31]{2,1,0:T(8,128)} %fusion.18), custom_call_target="Cholesky" | custom-call | tf_op jit(solution)/shard_map/jit(cholesky)/cholesky | solution.py:29
  855.1 11.7 %custom-call.10 = f32[64,1,31,31]{0,2,3,1:T(8,128)S(1)} custom-call(f32[64,1,31,31]{0,3,2,1:T(8,128)S(1)} %select_bitcast_fusion), custom_call_target="InvertDiagBlocksLowerTriangular" | custom-call | tf_op jit(solution)/shard_map/triangular_solve | solution.py:31
  867.8 13.7 %subtract_convert_fusion.1 = (bf16[1,64,64,512]{3,2,0,1:T(8,128)(2,1)S(1)}, bf16[1,64,64,512]{3,2,0,1:T(8,128)(2,1)}) fusion(f32[2,64,64,512]{3,2,0,1:T(8,128)} %copy_convert_fusion, f32[2,64,64,512]{3,2,0,1:T(8,128)} %convert_bitcast_fusion, f32[64,64]{1,0:T(8,128)S(1)} %convolution_negate_fusion, f32[64,64]{1,0:T(8,128)S(1)} %fusion.48), kind=kLoop, calls=%fused_computation.18 | loop fusion | flops 20971520 | bytes 41975808 | tf_op jit(solution)/shard_map/convert.2
  881.5 6.4 pad_maximum_fusion
  887.9 34.3 %copy.49 = bf16[2,64,64,512]{2,0,1,3:T(2,128)(2,1)} copy(bf16[2,64,64,512]{3,2,0,1:T(8,128)(2,1)} %pad_maximum_fusion) | data formatting | bytes 16777216 | tf_op jit(solution)/shard_map/stack | solution.py:95
  922.2 16.6 %reshape.205 = bf16[4,2,524288]{2,1,0:T(2,128)(2,1)} reshape(bf16[512,64,2,64]{3,2,1,0:T(2,128)(2,1)} %bitcast.133) | data formatting | bytes 16777216
  938.8 8.4 all-to-all-start
  947.1 2.2 multiply_convert_fusion.1
  949.4 91.6 %all-to-all-done = bf16[4,2,524288]{2,1,0:T(2,128)(2,1)} async-done(((bf16[4,2,524288]{2,1,0:T(2,128)(2,1)}), bf16[4,2,524288]{2,1,0:T(2,128)(2,1)}, u32[]{:S(2)}, u32[]{:S(2)}) %all-to-all-start) | async-done | bytes 8388640 | tf_op jit(solution)/shard_map/all_to_all | solution.py:97
  1041.0 16.0 %reshape.206 = bf16[512,64,2,64]{3,2,1,0:T(2,128)(2,1)} reshape(bf16[4,2,524288]{2,1,0:T(2,128)(2,1)} %all-to-all-done) | data formatting | bytes 16777216
  1056.9 34.3 %copy.50 = bf16[2,64,64,4,128]{4,2,1,3,0:T(8,128)(2,1)} copy(bf16[2,64,64,4,128]{2,0,1,4,3:T(2,128)(2,1)} %bitcast.134) | data formatting | bytes 16777216 | tf_op jit(solution)/shard_map/all_to_all | solution.py:97
  1091.2 23.6 %copy.80 = bf16[64,8,64,128]{3,1,2,0:T(8,128)(2,1)} copy(bf16[64,8,64,128]{3,2,1,0:T(8,128)(2,1)} %bitcast.135) | data formatting | bytes 16777216
  1114.9 12.0 %copy.51 = bf16[8192,512]{1,0:T(8,128)(2,1)} copy(bf16[8192,512]{0,1:T(8,128)(2,1)} %bitcast.136) | data formatting | bytes 16777216 | tf_op jit(solution)/shard_map/dot_general | solution.py:101
  1126.9 10.1 convolution_convert_fusion
  (53 shorter events, 15.7 us)
Async XLA Ops:
  7.2 573.1 %all-reduce.4.cloned.1.call-start = ((), (), s32[]{:S(2)}) async-start(), calls=%async_computation.1 | async-start | bytes 50331648 | tf_op jit(solution)/shard_map/psum | solution.py:15
  23.4 11.7 %copy-start.1 = (s32[64,512]{1,0:T(8,128)S(1)}, s32[64,512]{1,0:T(8,128)}, u32[]{:S(2)}) copy-start(s32[64,512]{1,0:T(8,128)} %param.4) | copy-start | bytes 393220
  41.4 3.1 slice-start
  41.8 4.0 slice-start.1
  605.7 10.2 copy-start
  867.1 14.4 %copy-start.2 = (f32[64,31]{0,1:T(8,128)}, f32[64,31]{0,1:T(8,128)S(1)}, u32[]{:S(2)}) copy-start(f32[64,31]{0,1:T(8,128)S(1)} %fusion.26) | copy-start | bytes 23812
  938.8 102.2 %all-to-all-start = ((bf16[4,2,524288]{2,1,0:T(2,128)(2,1)}), bf16[4,2,524288]{2,1,0:T(2,128)(2,1)}, u32[]{:S(2)}, u32[]{:S(2)}) async-start(bf16[4,2,524288]{2,1,0:T(2,128)(2,1)} %reshape.205), calls=%async_computation | async-start | bytes 16777216 | tf_op jit(solution)/shard_map/all_to_all | solution.py:97
Sparse Core Ops, SparseCore 0:
  21.6 558.5 all-reduce.3
where the time goes:
time: 1160 us; the launch traced here: 1140 us
  waiting for transfers between devices  602 us (52%)
  other arithmetic  265 us (23%)
  local copies, waits for them, and re-layouts  172 us (15%)
  matrix products  63.8 us (6%)
  between operations  18.6 us (2%)
  blocking collectives  13.8 us (1%)
    psum x1, waiting for transfers between devices, broadcast(): return lax.psum(kept, axis)  511 us
    another operation x4, other arithmetic, solve_filters(): factor = jnp.linalg.cholesky(normal)  182 us
    all_to_all x1, waiting for transfers between devices, per_device(): lax.all_to_all(residual, 'freq', split_axis=3, concat_axis=1, tiled=True)  91.6 us
    unnamed x14, local copies, waits for them, and re-layouts  69.1 us
    dot_general x3, matrix products, product_step(): jnp.einsum('cfsk,fkr->cfsr', stacked, right_side, preferred_element_type=...  41.3 us
    another operation x1, local copies, waits for them, and re-layouts, per_device(): residual = jnp.stack([res_real, res_imag]).astype(jnp.bfloat16)  34.3 us
    all_to_all x1, local copies, waits for them, and re-layouts, per_device(): lax.all_to_all(residual, 'freq', split_axis=3, concat_axis=1, tiled=True)  34.3 us
  transfers between devices with their start and end apart: 2, of which 2 were waited for; matrix products, arithmetic and copies ran while one was open for 4% of the time, Pallas kernels for 0%

commit v1 on v0

--- a/solution.py
+++ b/solution.py
@@ -94,7 +94,10 @@
     res_imag = data_wide[1] - (resp_real * pred_wide[1] + resp_imag * pred_wide[0])
     residual = jnp.stack([res_real, res_imag]).astype(jnp.bfloat16)
     full_table = band_table(jnp.arange(F, dtype=jnp.int32), F).reshape(2 * F, 2 * F)
-    shard_piece = lax.all_to_all(residual, "freq", split_axis=3, concat_axis=1, tiled=True)
+    shard_piece = jnp.concatenate(
+        lax.all_to_all(jnp.stack(jnp.split(residual, lax.axis_size("freq"), axis=3)), "freq", 0, 0),
+        axis=1,
+    )
     item_count = shard_piece.shape[2]
     recv_part = shard_piece.shape[3]
     flattened = shard_piece.reshape(2 * F, item_count * recv_part)

time: 1160 us -> 1060 us (0.914)
  local copies, waits for them, and re-layouts: 172 us -> 80.8 us
    another operation x1 -> x0, local copies, waits for them, and re-layouts: 34.3 us -> none  [per_device(): residual = jnp.stack([res_real, res_imag]).astype(jnp.bfloat16)]
    all_to_all x1 -> x0, local copies, waits for them, and re-layouts: 34.3 us -> none  [per_device(): lax.all_to_all(residual, 'freq', split_axis=3, concat_axis=1, tiled=True)]
    unnamed x14 -> x12, local copies, waits for them, and re-layouts: 69.1 us -> 36.4 us
  transfers between devices with their start and end apart: 2 -> 2, of which waited for: 2 -> 2; matrix products, arithmetic and copies ran while one was open for 4% -> 5% of each run, Pallas kernels for 0% -> 0%
where the time goes in v1:
time: 1060 us; the launch traced here: 1050 us
  waiting for transfers between devices  602 us (57%)
  other arithmetic  263 us (25%)
  local copies, waits for them, and re-layouts  80.8 us (8%)
  matrix products  63.4 us (6%)
  between operations  18.3 us (2%)
  blocking collectives  13.6 us (1%)
    psum x1, waiting for transfers between devices, broadcast(): return lax.psum(kept, axis)  511 us
    another operation x4, other arithmetic, solve_filters(): factor = jnp.linalg.cholesky(normal)  182 us
    all_to_all x1, waiting for transfers between devices, per_device(): lax.all_to_all(jnp.stack(jnp.split(residual, lax.axis_size('freq'), axis=...  91.2 us
    dot_general x3, matrix products, product_step(): jnp.einsum('cfsk,fkr->cfsr', stacked, right_side, preferred_element_type=...  41 us
    unnamed x12, local copies, waits for them, and re-layouts  36.4 us
  transfers between devices with their start and end apart: 2, of which 2 were waited for; matrix products, arithmetic and copies ran while one was open for 5% of the time, Pallas kernels for 0%

profile of v1, /device:TPU:1, one launch (start us, length us, event | category | flops | bytes accessed | tf_op | source)
XLA Modules:
  0.0 1049.0 jit_solution(16014030800375632436)
XLA Ops:
  7.2 1.4 fusion.88
  10.4 11.0 %broadcast_select_fusion.1 = (bf16[2,64,64,512]{3,2,1,0:T(8,128)(2,1)}, bf16[2,64,64,512]{3,2,1,0:T(8,128)(2,1)}, bf16[2,64,64,512]{3,2,1,0:T(8,128)(2,1)}) fusion(bf16[2,64,64,512]{3,2,1,0:T(8,128)(2,1)} %param.3, pred[]{:T(512)S(6)} %eq.69, pred[]{:T(512)S(6)} %eq.65, pred[]{:T(512)S(6)} %eq.73), kind=kLoop, calls=%fused_computation.35 | loop fusion | flops 12582912 | bytes 33554436 | tf_op jit(solution)/shard_map/jit(_where)/select_n | solution.py:14
  23.3 11.5 %copy.36 = bf16[2,64,64,512]{3,1,0,2:T(8,128)(2,1)} copy(bf16[2,64,64,512]{3,2,1,0:T(8,128)(2,1)} %param.3) | data formatting | bytes 16777216 | tf_op args[0]
  35.0 5.7 fusion.9
  42.8 1.5 pad_maximum_fusion.3
  44.4 1.3 slice-done.1
  45.7 2.3 fusion.8
  50.5 1.5 pad_maximum_fusion.2
  52.0 2.3 fusion.10
  56.4 1.5 pad_maximum_fusion.4
  57.9 11.7 %copy_convert_fusion = f32[2,64,64,512]{3,2,0,1:T(8,128)} fusion(bf16[2,64,64,512]{3,2,1,0:T(8,128)(2,1)} %param.3), kind=kLoop, calls=%fused_computation.22 | loop fusion | flops 4194304 | bytes 25165824 | tf_op jit(solution)/shard_map/convert_element_type | solution.py:76
  69.6 510.6 %all-reduce.4.cloned.1.call-done = (bf16[2,64,64,512]{3,2,1,0:T(8,128)(2,1)}, bf16[2,64,64,512]{3,2,1,0:T(8,128)(2,1)}, bf16[2,64,64,512]{3,2,1,0:T(8,128)(2,1)}) async-done(((bf16[2,64,64,512]{3,2,1,0:T(8,128)(2,1)}, bf16[2,64,64,512]{3,2,1,0:T(8,128)(2,1)}, bf16[2,64,64,512]{3,2,1,0:T(8,128)(2,1)}), (bf16[2,64,64,512]{3,2,1,0:T(8,128)(2,1)}, bf16[2,64,64,512]{3,2,1,0:T(8,128)(2,1)}, ...) | async-done | bytes 25165840 | tf_op jit(solution)/shard_map/psum | solution.py:15
  580.2 4.0 slice_bitcast_fusion.5
  584.2 11.2 %slice_bitcast_fusion.1 = (bf16[64,64,512]{2,1,0:T(8,128)(2,1)}, bf16[64,64,512]{2,1,0:T(8,128)(2,1)}, bf16[64,64,512]{2,1,0:T(8,128)(2,1)S(1)}, bf16[64,64,512]{2,1,0:T(8,128)(2,1)}) fusion(bf16[2,64,64,512]{3,2,1,0:T(8,128)(2,1)} %get-tuple-element.7, bf16[2,64,64,512]{3,2,1,0:T(8,128)(2,1)} %get-tuple-element.9), kind=kLoop, calls=%fused_computation.39 | loop fusion | bytes 33554432 | tf_op jit(solution)/shard_map/squeeze | solution.py:61
  595.3 10.3 fusion.3
  605.6 9.9 fusion
  615.5 20.8 %convert_bitcast_fusion = f32[2,64,64,512]{3,2,0,1:T(8,128)} fusion(bf16[64,64,512]{2,1,0:T(8,128)(2,1)} %get-tuple-element.21, bf16[64,64,512]{2,1,0:T(8,128)(2,1)S(1)} %copy-done, f32[64,512,2,64]{1,3,2,0:T(8,128)} %fusion, f32[64,512,2,64]{1,3,2,0:T(8,128)} %fusion.3, bf16[2,64,64,128]{3,1,2,0:T(8,128)(2,1)} %pad_maximum_fusion.4), kind=kOutput, calls=%fused_computation.1 | convolution fusion | flops 1111490560 | bytes 60817408 | tf_op jit(solution)/shard_map/cfsk,fkr->cfsr/dot_general | solution.py:62
  636.3 13.9 %subtract_reduce_fusion = (f32[64,64]{1,0:T(8,128)S(1)}, f32[64,64]{1,0:T(8,128)S(1)}, f32[64,64]{1,0:T(8,128)S(1)}) fusion(f32[2,64,64,512]{3,2,0,1:T(8,128)} %copy_convert_fusion, f32[2,64,64,512]{3,2,0,1:T(8,128)} %convert_bitcast_fusion), kind=kLoop, calls=%fused_computation.25 | loop fusion | flops 25153536 | bytes 33603584 | tf_op jit(solution)/shard_map/reduce_sum | solution.py:79
  651.5 13.6 %all-reduce = (f32[64,31]{0,1:T(8,128)S(1)}, f32[64,31]{0,1:T(8,128)S(1)}) all-reduce(f32[64,31]{0,1:T(8,128)S(1)} %fusion.40, f32[64,31]{0,1:T(8,128)S(1)} %convolution_subtract_fusion), channel_id=1, replica_groups=mesh['shot'=32,'freq'=4] {'freq'}, use_global_device_ids=true, to_apply=%region_4.5 | all-reduce | flops 3968 | bytes 31744 | tf_op jit(solution)/shard_map/psum | solution.py:89
  665.0 2.9 gather_fusion
  671.1 182.3 %custom-call.9 = f32[64,31,31]{2,1,0:T(8,128)S(1)} custom-call(f32[64,31,31]{2,1,0:T(8,128)} %fusion.25), custom_call_target="Cholesky" | custom-call | tf_op jit(solution)/shard_map/jit(cholesky)/cholesky | solution.py:29
  854.5 11.7 %custom-call.10 = f32[64,1,31,31]{0,2,3,1:T(8,128)S(1)} custom-call(f32[64,1,31,31]{0,3,2,1:T(8,128)S(1)} %select_bitcast_fusion), custom_call_target="InvertDiagBlocksLowerTriangular" | custom-call | tf_op jit(solution)/shard_map/triangular_solve | solution.py:31
  867.2 11.6 %subtract_convert_fusion.1 = (bf16[1,64,64,512]{3,2,0,1:T(8,128)(2,1)S(1)}, bf16[1,64,64,512]{3,2,0,1:T(8,128)(2,1)S(1)}) fusion(f32[2,64,64,512]{3,2,0,1:T(8,128)} %copy_convert_fusion, f32[2,64,64,512]{3,2,0,1:T(8,128)} %convert_bitcast_fusion, f32[64,64]{1,0:T(8,128)S(1)} %convolution_negate_fusion, f32[64,64]{1,0:T(8,128)S(1)} %fusion.55), kind=kLoop, calls=%fused_computation.24 | loop fusion | flops 20971520 | bytes 41975808 | tf_op jit(solution)/shard_map/convert.2
  878.8 1.7 fusion.17
  880.6 3.9 pad_maximum_fusion
  884.4 8.4 all-to-all-start
  892.8 2.6 multiply_convert_fusion.1
  895.5 91.2 %all-to-all-done = bf16[4,2,64,64,128]{4,3,1,2,0:T(8,128)(2,1)} async-done(((bf16[4,2,64,64,128]{4,3,1,2,0:T(8,128)(2,1)}), bf16[4,2,64,64,128]{4,3,1,2,0:T(8,128)(2,1)}, u32[]{:S(2)}, u32[]{:S(2)}) %all-to-all-start) | async-done | bytes 8388640 | tf_op jit(solution)/shard_map/all_to_all | solution.py:98
  986.7 9.7 copy.49
  996.3 23.6 %copy.79 = bf16[64,8,64,128]{3,1,2,0:T(8,128)(2,1)} copy(bf16[64,8,64,128]{3,2,1,0:T(8,128)(2,1)} %bitcast.138) | data formatting | bytes 16777216
  1019.9 12.0 %copy.50 = bf16[8192,512]{1,0:T(8,128)(2,1)} copy(bf16[8192,512]{0,1:T(8,128)(2,1)} %bitcast.139) | data formatting | bytes 16777216 | tf_op jit(solution)/shard_map/dot_general | solution.py:104
  1031.9 10.1 convolution_convert_fusion
  (51 shorter events, 13.2 us)
Async XLA Ops:
  7.2 573.0 %all-reduce.4.cloned.1.call-start = ((), (), s32[]{:S(2)}) async-start(), calls=%async_computation.1 | async-start | bytes 50331648 | tf_op jit(solution)/shard_map/psum | solution.py:15
  23.2 11.7 %copy-start.1 = (s32[64,512]{1,0:T(8,128)S(1)}, s32[64,512]{1,0:T(8,128)}, u32[]{:S(2)}) copy-start(s32[64,512]{1,0:T(8,128)} %param.4) | copy-start | bytes 393220
  41.3 3.1 slice-start
  41.7 4.0 slice-start.1
  605.6 9.9 copy-start
  866.5 12.4 %copy-start.2 = (f32[64,31]{0,1:T(8,128)}, f32[64,31]{0,1:T(8,128)S(1)}, u32[]{:S(2)}) copy-start(f32[64,31]{0,1:T(8,128)S(1)} %fusion.33) | copy-start | bytes 23812
  884.4 102.2 %all-to-all-start = ((bf16[4,2,64,64,128]{4,3,1,2,0:T(8,128)(2,1)}), bf16[4,2,64,64,128]{4,3,1,2,0:T(8,128)(2,1)}, u32[]{:S(2)}, u32[]{:S(2)}) async-start(bf16[4,2,64,64,128]{4,3,1,2,0:T(8,128)(2,1)} %pad_maximum_fusion), calls=%async_computation | async-start | bytes 16777216 | tf_op jit(solution)/shard_map/all_to_all | solution.py:98
Sparse Core Ops, SparseCore 0:
  21.5 558.5 all-reduce.3
